TPU v7x, 32 devices: a whole 2x2x4 slice. The times are simulated.
32 devices in a mesh: rows: 8 (over y, x, core), grp: 4 (over z).
Axes of the slice: x: 2, y: 2, z: 4, core: 2. Of those that a mesh axis runs over, the one named last changes fastest.
Arguments:
- date_keys: int32 [262144], P(('rows', 'grp')), may hold values from 0 to 2559
- product_keys: int32 [262144], P(('rows', 'grp')), may hold values from 0 to 16255
- quantity: float32 [262144], P(('rows', 'grp')), may hold values from 0.01 to 10
- date_flags: int32 [2560], P('rows'), may hold values 0 or 1
- category: int32 [16256], P('rows'), may hold values from 0 to 999
- unit_price: float32 [16256], P('rows'), may hold values from 0.5 to 4
- unit_cost: float32 [16256], P('rows'), may hold values from 0.25 to 2
Outputs:
- revenue_by_category: float32 [1000], replicated
- profit_by_category: float32 [1000], replicated
All inputs are finite; a program needn't handle non-finite values. No bound on the sum of `date_flags` on one device may be relied on, other than what follows from the above.
Results may differ from a plain program's by a relative error of at most 0.00005.
Values sent between devices are 32-bit elements; how exact they have to be, the bound alone decides.
A program may use at most 192 MiB of HBM per device.

v0:
```python
import jax
import jax.numpy as jnp
from jax import lax
from jax.sharding import PartitionSpec as P

CATS = 1000


def category_sums(group_ids, amounts):
    length = group_ids.shape[0]
    padded = (CATS + 127) // 128 * 128
    block_rows = min(2048, (length + 127) // 128 * 128)
    total_rows = (length + block_rows - 1) // block_rows * block_rows
    extra = total_rows - length
    group_ids = jnp.concatenate([group_ids, jnp.full((extra,), padded, jnp.int32)])
    amounts = jnp.concatenate([amounts, jnp.zeros((2, extra), jnp.float32)], axis=1)
    columns = lax.broadcasted_iota(jnp.int32, (block_rows, padded), 1)

    def add_block(running, pieces):
        block_ids, block_amounts = pieces
        onehot = (block_ids[:, None] == columns).astype(jnp.float32)
        summed = jnp.dot(
            block_amounts,
            onehot,
            precision=lax.Precision.HIGHEST,
            preferred_element_type=jnp.float32,
        )
        return (running + summed, None)

    stacked = amounts.reshape(2, total_rows // block_rows, block_rows).transpose(1, 0, 2)
    running, _ = lax.scan(
        add_block, jnp.zeros((2, padded), jnp.float32), (group_ids.reshape(-1, block_rows), stacked)
    )
    return running


def window_sums(product_keys, kept_amount, row_count):
    inside = (product_keys >= 0) & (product_keys < row_count)
    segment = jnp.where(inside, product_keys, row_count)
    summed = jax.ops.segment_sum(
        jnp.where(inside, kept_amount, 0.0), segment, num_segments=row_count + 1
    )
    return summed[:row_count]


def body(date_keys, product_keys, quantity, date_flags, category, unit_price, unit_cost):
    date_mask = lax.all_gather(date_flags, "rows", axis=0, tiled=True)
    passed = jnp.take(date_mask, date_keys, axis=0)
    kept_amount = jnp.where(passed == 1, quantity, 0.0)
    shard_len = unit_price.shape[0]
    amount = lax.psum_scatter(
        window_sums(product_keys, kept_amount, shard_len * lax.axis_size("rows")),
        "rows",
        scatter_dimension=0,
        tiled=True,
    )
    revenue = amount * unit_price
    profit = amount * (unit_price - unit_cost)
    partial_value = category_sums(category, jnp.stack([revenue, profit]))
    totals = lax.psum(partial_value, ("rows", "grp"))
    fact_total = date_keys.shape[0] * lax.axis_size("rows") * lax.axis_size("grp")
    factor = CATS / fact_total
    return (totals[0, :CATS] * factor, totals[1, :CATS] * factor)


def solution(mesh):
    return jax.shard_map(
        body,
        mesh=mesh,
        in_specs=(
            P(("rows", "grp")),
            P(("rows", "grp")),
            P(("rows", "grp")),
            P("rows"),
            P("rows"),
            P("rows"),
            P("rows"),
        ),
        out_specs=(P(), P()),
        check_vma=False,
    )
```

profile of v0, /device:TPU:0, one launch (start us, length us, event | category | flops | bytes accessed | tf_op | source)
XLA Modules:
  0.0 184.5 jit_solution(4197366333144670196)
XLA Ops:
  0.6 0.0 copy-start
  0.7 1.3 fusion.16
  2.6 0.9 dynamic-update-slice
  3.5 25.5 %all-reduce.2 = s32[2560]{0:T(1024)S(1)} all-reduce(s32[2560]{0:T(1024)S(1)} %dynamic-update-slice), channel_id=1, replica_groups=mesh['rows'=8,'grp'=4] {'rows'}, use_global_device_ids=true, to_apply=%add.2 | all-reduce | flops 2560 | bytes 20480
  29.1 0.0 copy-done
  29.1 0.0 copy-start.1
  29.1 0.0 copy-start.2
  29.1 45.5 %gather_fusion = s32[8192]{0:T(1024)S(1)} fusion(s32[2560]{0:T(1024)S(1)} %all-reduce.2, s32[8192]{0:T(1024)S(1)} %fusion.4), kind=kCustom, calls=%fused_computation | custom fusion | bytes 98304 | tf_op jit(solution)/shard_map/jit(_take)/gather | solution.py:48
  74.6 0.0 copy-done.1
  74.7 0.0 copy-done.2
  74.7 43.2 %scatter_custom_fusion = f32[16257]{0:T(1024)S(1)} fusion(s32[8192]{0:T(1024)S(1)} %fusion.5, f32[8192]{0:T(1024)S(1)} %select_select_fusion, f32[]{:T(128)} %constant.10.clone.1), kind=kCustom, calls=%fused_computation.8 | custom fusion | flops 8192 | bytes 65032 | tf_op jit(solution)/shard_map/scatter-add | solution.py:40
  117.9 0.0 copy-start.4
  118.0 0.0 copy-start.5
  118.0 0.0 copy-start.3
  118.0 22.9 %all-reduce.3 = f32[16256]{0:T(1024)S(1)} all-reduce(f32[16256]{0:T(1024)S(1)} %bitcast.7), channel_id=2, replica_groups=mesh['rows'=8,'grp'=4] {'rows'}, use_global_device_ids=true, to_apply=%region_1.2.clone | all-reduce | flops 16256 | bytes 130048
  141.5 0.0 copy-done.4
  141.5 0.0 copy-done.5
  141.5 0.1 dynamic-slice_multiply_fusion
  141.6 0.0 copy-done.3
  141.6 2.7 %fusion = f32[2,1024]{1,0:T(2,128)S(1)} fusion(s32[2048]{0:T(1024)S(1)} %concatenate.7, f32[1,2032]{1,0:T(1,128)S(1)} %bitcast.9, f32[1,2032]{1,0:T(1,128)S(1)} %bitcast.8), kind=kOutput, calls=%fused_computation.3 | convolution fusion | flops 52445184 | bytes 32640 | tf_op jit(solution)/shard_map/while/body/eval_jaxpr/dot_general | solution.py:22
  144.4 39.5 %psum.7 = f32[2,1024]{1,0:T(2,128)S(1)} all-reduce(f32[2,1024]{1,0:T(2,128)S(1)} %fusion), channel_id=1, replica_groups=mesh['rows'=8,'grp'=4] {'rows','grp'}, use_global_device_ids=true, to_apply=%region_2.3 | all-reduce | flops 2048 | bytes 16384 | tf_op jit(solution)/shard_map/psum | solution.py:60
  183.9 0.6 slice_multiply_fusion
  (5 shorter events, 0.0 us)
Async XLA Ops:
  0.6 28.4 %copy-start = (s32[8192]{0:T(1024)S(1)}, s32[8192]{0:T(1024)}, u32[]{:S(2)}) copy-start(s32[8192]{0:T(1024)} %param.7) | copy-start | bytes 98308
  29.1 45.6 %copy-start.1 = (s32[8192]{0:T(1024)S(1)}, s32[8192]{0:T(1024)}, u32[]{:S(2)}) copy-start(s32[8192]{0:T(1024)} %param.8) | copy-start | bytes 98308
  29.1 45.6 %copy-start.2 = (f32[8192]{0:T(1024)S(1)}, f32[8192]{0:T(1024)}, u32[]{:S(2)}) copy-start(f32[8192]{0:T(1024)} %param.9) | copy-start | bytes 98308
  117.9 23.6 %copy-start.4 = (f32[2032]{0:T(1024)S(1)}, f32[2032]{0:T(1024)}, u32[]{:S(2)}) copy-start(f32[2032]{0:T(1024)} %param.12) | copy-start | bytes 24388
  118.0 23.6 %copy-start.5 = (f32[2032]{0:T(1024)S(1)}, f32[2032]{0:T(1024)}, u32[]{:S(2)}) copy-start(f32[2032]{0:T(1024)} %param.13) | copy-start | bytes 24388
  118.0 23.6 %copy-start.3 = (s32[2032]{0:T(1024)S(1)}, s32[2032]{0:T(1024)}, u32[]{:S(2)}) copy-start(s32[2032]{0:T(1024)} %param.11) | copy-start | bytes 24388
where the time goes:
time: 185 us
  blocking collectives  87.9 us (48%)
  local copies, waits for them, and re-layouts  47.8 us (26%)
  other arithmetic  44 us (24%)
  matrix products  2.74 us (1%)
  between operations  2.08 us (1%)
    unnamed x2, blocking collectives  48.4 us
    gather x1, local copies, waits for them, and re-layouts, body(): passed = jnp.take(date_mask, date_keys, axis=0)  45.5 us
    scatter-add x1, other arithmetic, window_sums(): jax.ops.segment_sum(jnp.where(inside, kept_amount, 0.0), segment, num_seg...  43.2 us
    psum x1, blocking collectives, body(): totals = lax.psum(partial_value, ('rows', 'grp'))  39.5 us

commit v1 on v0

--- a/solution.py
+++ b/solution.py
@@ -57,7 +57,7 @@
     revenue = amount * unit_price
     profit = amount * (unit_price - unit_cost)
     partial_value = category_sums(category, jnp.stack([revenue, profit]))
-    totals = lax.psum(partial_value, ("rows", "grp"))
+    totals = jnp.sum(lax.all_gather(partial_value, ("rows", "grp")), axis=0)
     fact_total = date_keys.shape[0] * lax.axis_size("rows") * lax.axis_size("grp")
     factor = CATS / fact_total
     return (totals[0, :CATS] * factor, totals[1, :CATS] * factor)

time: 185 us -> 215 us (1.16)
  blocking collectives: 87.9 us -> 117 us
    all_gather x0 -> x1, blocking collectives: none -> 68.6 us  [body(): totals = jnp.sum(lax.all_gather(partial_value, ('rows', 'grp')), axis=0)]
    psum x1 -> x0, blocking collectives: 39.5 us -> none  [body(): totals = lax.psum(partial_value, ('rows', 'grp'))]
where the time goes in v1:
time: 215 us
  blocking collectives  117 us (54%)
  local copies, waits for them, and re-layouts  48.5 us (23%)
  other arithmetic  44.8 us (21%)
  matrix products  2.74 us (1%)
    all_gather x1, blocking collectives, body(): totals = jnp.sum(lax.all_gather(partial_value, ('rows', 'grp')), axis=0)  68.6 us
    unnamed x2, blocking collectives  48.3 us
    gather x1, local copies, waits for them, and re-layouts, body(): passed = jnp.take(date_mask, date_keys, axis=0)  45.5 us
    scatter-add x1, other arithmetic, window_sums(): jax.ops.segment_sum(jnp.where(inside, kept_amount, 0.0), segment, num_seg...  43.2 us

profile of v1, /device:TPU:0, one launch (start us, length us, event | category | flops | bytes accessed | tf_op | source)
XLA Modules:
  0.0 214.9 jit_solution(8552686019833655639)
XLA Ops:
  0.6 1.3 fusion.17
  3.3 0.7 concatenate.7
  4.0 0.9 dynamic-update-slice
  4.8 25.5 %all-reduce.2 = s32[2560]{0:T(1024)S(1)} all-reduce(s32[2560]{0:T(1024)S(1)} %dynamic-update-slice), channel_id=1, replica_groups=mesh['rows'=8,'grp'=4] {'rows'}, use_global_device_ids=true, to_apply=%add.2 | all-reduce | flops 2560 | bytes 20480
  30.4 0.8 fusion.5
  31.1 0.0 copy-start
  31.1 0.0 copy-start.1
  31.1 0.0 copy-start.2
  31.2 45.5 %gather_fusion = s32[8192]{0:T(1024)S(1)} fusion(s32[2560]{0:T(1024)S(1)} %all-reduce.2, s32[8192]{0:T(1024)S(1)} %fusion.5), kind=kCustom, calls=%fused_computation | custom fusion | bytes 98304 | tf_op jit(solution)/shard_map/jit(_take)/gather | solution.py:48
  76.7 0.0 copy-done
  76.7 0.0 copy-done.1
  76.7 0.0 copy-done.2
  76.7 0.0 copy-start.3
  76.7 0.0 copy-start.4
  76.8 43.2 %scatter_custom_fusion = f32[16257]{0:T(1024)S(1)} fusion(s32[8192]{0:T(1024)S(1)} %fusion.6, f32[8192]{0:T(1024)S(1)} %select_select_fusion, f32[]{:T(128)} %constant.10.clone.1), kind=kCustom, calls=%fused_computation.9 | custom fusion | flops 8192 | bytes 65032 | tf_op jit(solution)/shard_map/scatter-add | solution.py:40
  120.0 22.7 %all-reduce.3 = f32[16256]{0:T(1024)S(1)} all-reduce(f32[16256]{0:T(1024)S(1)} %bitcast.9), channel_id=3, replica_groups=mesh['rows'=8,'grp'=4] {'rows'}, use_global_device_ids=true, to_apply=%region_1.2.clone | all-reduce | flops 16256 | bytes 130048
  142.8 0.0 copy-done.3
  142.8 0.0 copy-done.4
  142.8 0.1 dynamic-slice_multiply_fusion
  142.9 2.7 %fusion.2 = f32[1,2,1024]{2,1,0:T(2,128)S(1)} fusion(s32[2048]{0:T(1024)S(1)} %concatenate.7, f32[1,2032]{1,0:T(1,128)S(1)} %bitcast.11, f32[1,2032]{1,0:T(1,128)S(1)} %bitcast.10), kind=kOutput, calls=%fused_computation.5 | convolution fusion | flops 52445184 | bytes 32640 | tf_op jit(solution)/shard_map/while/body/eval_jaxpr/dot_general | solution.py:22
  145.6 68.6 %all-gather.1 = f32[32,2,1024]{2,1,0:T(2,128)S(1)} all-gather(f32[1,2,1024]{2,1,0:T(2,128)S(1)} %fusion.2), channel_id=2, replica_groups=mesh['rows'=8,'grp'=4] {'rows','grp'}, dimensions={0}, use_global_device_ids=true | all-gather | bytes 270336 | tf_op jit(solution)/shard_map/all_gather | solution.py:60
  214.2 0.1 reduce_sum.9
  214.3 0.6 slice_multiply_fusion
  (3 shorter events, 0.0 us)
Async XLA Ops:
  31.1 45.6 %copy-start = (s32[8192]{0:T(1024)S(1)}, s32[8192]{0:T(1024)}, u32[]{:S(2)}) copy-start(s32[8192]{0:T(1024)} %param.7) | copy-start | bytes 98308
  31.1 45.6 %copy-start.1 = (s32[8192]{0:T(1024)S(1)}, s32[8192]{0:T(1024)}, u32[]{:S(2)}) copy-start(s32[8192]{0:T(1024)} %param.8) | copy-start | bytes 98308
  31.1 45.6 %copy-start.2 = (f32[8192]{0:T(1024)S(1)}, f32[8192]{0:T(1024)}, u32[]{:S(2)}) copy-start(f32[8192]{0:T(1024)} %param.9) | copy-start | bytes 98308
  76.7 66.0 %copy-start.3 = (f32[2032]{0:T(1024)S(1)}, f32[2032]{0:T(1024)}, u32[]{:S(2)}) copy-start(f32[2032]{0:T(1024)} %param.12) | copy-start | bytes 24388
  76.7 66.0 %copy-start.4 = (f32[2032]{0:T(1024)S(1)}, f32[2032]{0:T(1024)}, u32[]{:S(2)}) copy-start(f32[2032]{0:T(1024)} %param.13) | copy-start | bytes 24388

commit v2 on v0

--- a/solution.py
+++ b/solution.py
@@ -57,7 +57,7 @@
     revenue = amount * unit_price
     profit = amount * (unit_price - unit_cost)
     partial_value = category_sums(category, jnp.stack([revenue, profit]))
-    totals = lax.psum(partial_value, ("rows", "grp"))
+    totals = lax.psum(lax.psum(partial_value, "grp"), "rows")
     fact_total = date_keys.shape[0] * lax.axis_size("rows") * lax.axis_size("grp")
     factor = CATS / fact_total
     return (totals[0, :CATS] * factor, totals[1, :CATS] * factor)

time: 185 us -> 170 us (0.919)
  blocking collectives: 87.9 us -> 72.6 us
    psum x1 -> x2, blocking collectives: 39.5 us -> 24.2 us  [body(): totals = lax.psum(lax.psum(partial_value, 'grp'), 'rows')]
where the time goes in v2:
time: 170 us; the launch traced here: 169 us
  blocking collectives  72.6 us (43%)
  local copies, waits for them, and re-layouts  47.8 us (28%)
  other arithmetic  44 us (26%)
  matrix products  2.74 us (2%)
  between operations  2.09 us (1%)
    unnamed x2, blocking collectives  48.4 us
    gather x1, local copies, waits for them, and re-layouts, body(): passed = jnp.take(date_mask, date_keys, axis=0)  45.5 us
    scatter-add x1, other arithmetic, window_sums(): jax.ops.segment_sum(jnp.where(inside, kept_amount, 0.0), segment, num_seg...  43.2 us
    psum x2, blocking collectives, body(): totals = lax.psum(lax.psum(partial_value, 'grp'), 'rows')  24.2 us

profile of v2, /device:TPU:0, one launch (start us, length us, event | category | flops | bytes accessed | tf_op | source)
XLA Modules:
  0.0 169.2 jit_solution(14713599832865144725)
XLA Ops:
  0.6 0.0 copy-start
  0.7 1.3 fusion.16
  2.6 0.9 dynamic-update-slice
  3.5 25.5 %all-reduce.2 = s32[2560]{0:T(1024)S(1)} all-reduce(s32[2560]{0:T(1024)S(1)} %dynamic-update-slice), channel_id=1, replica_groups=mesh['rows'=8,'grp'=4] {'rows'}, use_global_device_ids=true, to_apply=%add.2 | all-reduce | flops 2560 | bytes 20480
  29.1 0.0 copy-done
  29.1 0.0 copy-start.1
  29.1 0.0 copy-start.2
  29.1 45.5 %gather_fusion = s32[8192]{0:T(1024)S(1)} fusion(s32[2560]{0:T(1024)S(1)} %all-reduce.2, s32[8192]{0:T(1024)S(1)} %fusion.4), kind=kCustom, calls=%fused_computation | custom fusion | bytes 98304 | tf_op jit(solution)/shard_map/jit(_take)/gather | solution.py:48
  74.6 0.0 copy-done.1
  74.7 0.0 copy-done.2
  74.7 43.2 %scatter_custom_fusion = f32[16257]{0:T(1024)S(1)} fusion(s32[8192]{0:T(1024)S(1)} %fusion.5, f32[8192]{0:T(1024)S(1)} %select_select_fusion, f32[]{:T(128)} %constant.10.clone.1), kind=kCustom, calls=%fused_computation.8 | custom fusion | flops 8192 | bytes 65032 | tf_op jit(solution)/shard_map/scatter-add | solution.py:40
  117.9 0.0 copy-start.4
  118.0 0.0 copy-start.5
  118.0 0.0 copy-start.3
  118.0 22.9 %all-reduce.3 = f32[16256]{0:T(1024)S(1)} all-reduce(f32[16256]{0:T(1024)S(1)} %bitcast.7), channel_id=2, replica_groups=mesh['rows'=8,'grp'=4] {'rows'}, use_global_device_ids=true, to_apply=%region_1.2.clone | all-reduce | flops 16256 | bytes 130048
  141.5 0.0 copy-done.4
  141.5 0.0 copy-done.5
  141.5 0.1 dynamic-slice_multiply_fusion
  141.6 0.0 copy-done.3
  141.6 2.7 %fusion = f32[2,1024]{1,0:T(2,128)S(1)} fusion(s32[2048]{0:T(1024)S(1)} %concatenate.7, f32[1,2032]{1,0:T(1,128)S(1)} %bitcast.9, f32[1,2032]{1,0:T(1,128)S(1)} %bitcast.8), kind=kOutput, calls=%fused_computation.3 | convolution fusion | flops 52445184 | bytes 32640 | tf_op jit(solution)/shard_map/while/body/eval_jaxpr/dot_general | solution.py:22
  144.4 12.1 %psum.14 = f32[2,1024]{1,0:T(2,128)S(1)} all-reduce(f32[2,1024]{1,0:T(2,128)S(1)} %fusion), channel_id=1, replica_groups=mesh['rows'=8,'grp'=4] {'grp'}, use_global_device_ids=true, to_apply=%region_2.3 | all-reduce | flops 2048 | bytes 16384 | tf_op jit(solution)/shard_map/psum | solution.py:60
  156.5 12.1 %psum.15 = f32[2,1024]{1,0:T(2,128)S(1)} all-reduce(f32[2,1024]{1,0:T(2,128)S(1)} %psum.14), channel_id=1, replica_groups=mesh['rows'=8,'grp'=4] {'rows'}, use_global_device_ids=true, to_apply=%region_3.4 | all-reduce | flops 2048 | bytes 16384 | tf_op jit(solution)/shard_map/psum | solution.py:60
  168.6 0.6 slice_multiply_fusion
  (5 shorter events, 0.0 us)
Async XLA Ops:
  0.6 28.4 %copy-start = (s32[8192]{0:T(1024)S(1)}, s32[8192]{0:T(1024)}, u32[]{:S(2)}) copy-start(s32[8192]{0:T(1024)} %param.7) | copy-start | bytes 98308
  29.1 45.6 %copy-start.1 = (s32[8192]{0:T(1024)S(1)}, s32[8192]{0:T(1024)}, u32[]{:S(2)}) copy-start(s32[8192]{0:T(1024)} %param.8) | copy-start | bytes 98308
  29.1 45.6 %copy-start.2 = (f32[8192]{0:T(1024)S(1)}, f32[8192]{0:T(1024)}, u32[]{:S(2)}) copy-start(f32[8192]{0:T(1024)} %param.9) | copy-start | bytes 98308
  117.9 23.6 %copy-start.4 = (f32[2032]{0:T(1024)S(1)}, f32[2032]{0:T(1024)}, u32[]{:S(2)}) copy-start(f32[2032]{0:T(1024)} %param.12) | copy-start | bytes 24388
  118.0 23.6 %copy-start.5 = (f32[2032]{0:T(1024)S(1)}, f32[2032]{0:T(1024)}, u32[]{:S(2)}) copy-start(f32[2032]{0:T(1024)} %param.13) | copy-start | bytes 24388
  118.0 23.6 %copy-start.3 = (s32[2032]{0:T(1024)S(1)}, s32[2032]{0:T(1024)}, u32[]{:S(2)}) copy-start(s32[2032]{0:T(1024)} %param.11) | copy-start | bytes 24388
